TPU v7x, 256 devices: a whole 4x4x8 slice. The times are simulated.
256 devices in a mesh: freq: 2 (over y_hi), row: 4 (over y_lo, core), blk: 32 (over x, z).
Axes of the slice: x: 4, y: 4 (y_hi: 2, y_lo: 2; y = y_hi * 2 + y_lo), z: 8, core: 2. Of those that a mesh axis runs over, the one named last changes fastest.
Arguments:
- counts: int32 [65536, 8, 128], P(('freq', 'row', 'blk')), parts along dimension 0, may hold values from 0 to 28, as said below
- subspace: bfloat16 [65536, 32], P(('freq', 'row', 'blk')), parts along dimension 0, may hold values from -6 to 6
Outputs:
- modes: float32 [65536, 32], P(('freq', 'row', 'blk')), parts along dimension 0
There are 2 independent parts, one for each index of `freq`. A program takes and returns all parts, laid end to end along the dimension named above; each array names one. Nothing has to cross between parts.
Inputs may be any that keep to these rules, and one draw needn't show every extreme that they name: Integer spike counts.
All inputs are finite; a program needn't handle non-finite values.
Results may differ from a plain program's by a relative error of at most 0.008.
Values may be sent and summed in bfloat16 or wider, within the bound.
No kernel may reach another device: no remote copies, remote signals or barrier semaphores. Data moves between devices by JAX's collectives and lax.ppermute only.
A program may use at most 64 MiB of HBM per device.

v0:
```python
import math
import jax
import jax.numpy as jnp
from jax import lax
from jax.sharding import PartitionSpec as P

SEGS = 8
TAPERS = 8
EPOCH_STEPS = 128
SPECTRAL_SLOT = 9
MODES = 32


def spectral_table():
    clock_moments = jnp.arange(EPOCH_STEPS, dtype=jnp.float32)
    window_degrees = jnp.arange(TAPERS, dtype=jnp.float32) + 1.0
    prolate_windows = jnp.sqrt(2.0 / (EPOCH_STEPS + 1.0)) * jnp.sin(
        jnp.pi * (clock_moments[:, None] + 1.0) * window_degrees[None, :] / (EPOCH_STEPS + 1.0)
    )
    oscillation_radians = 2.0 * jnp.pi * SPECTRAL_SLOT * clock_moments / EPOCH_STEPS
    return jnp.concatenate(
        [
            prolate_windows * jnp.cos(oscillation_radians)[:, None],
            -prolate_windows * jnp.sin(oscillation_radians)[:, None],
        ],
        axis=1,
    )


def make_spectra(counts):
    values = counts.astype(jnp.float32)
    centered = values - jnp.mean(values, axis=2, keepdims=True)
    height = counts.shape[0]
    flattened = centered.reshape(height * SEGS, EPOCH_STEPS)
    result = jnp.dot(
        flattened,
        spectral_table(),
        precision=lax.Precision.HIGHEST,
        preferred_element_type=jnp.float32,
    )
    return result.reshape(height, SEGS * 2 * TAPERS).astype(jnp.bfloat16)


def twist(spectra):
    height = spectra.shape[0]
    pieces_view = spectra.reshape(height, SEGS, 2, TAPERS)
    return jnp.stack([pieces_view[:, :, 1], -pieces_view[:, :, 0]], axis=2).reshape(
        height, SEGS * 2 * TAPERS
    )


def inverse_power(spectra):
    widened = spectra.astype(jnp.float32)
    return 1.0 / (jnp.sum(widened * widened, axis=1) + 1e-05)


def tile_image(stacked, inverse_rows, column_spectra, inverse_cols, column_subspace):
    height = inverse_rows.shape[0]
    products = lax.dot_general(
        stacked, column_spectra, (((1,), (1,)), ((), ())), preferred_element_type=jnp.float32
    )
    real_part = products[:height]
    imag_part = products[height:]
    squared = (
        (real_part * real_part + imag_part * imag_part)
        * inverse_rows[:, None]
        * inverse_cols[None, :]
    )
    degrees = float(SEGS * TAPERS)
    coherence = jnp.maximum((degrees * squared - 1.0) / (degrees - 1.0), 0.0).astype(jnp.bfloat16)
    return jnp.dot(coherence, column_subspace, preferred_element_type=jnp.float32)


def fold_pieces(accumulated, stacked, inverse_rows, pieces):
    column_spectra, column_subspace = pieces
    row_count = column_spectra.shape[0]
    rows_per_block = math.gcd(row_count, 2048)
    turns = row_count // rows_per_block

    def add_block(position, running):
        offset = position * rows_per_block
        spectra_here = lax.dynamic_slice_in_dim(column_spectra, offset, rows_per_block, 0)
        subspace_here = lax.dynamic_slice_in_dim(column_subspace, offset, rows_per_block, 0)
        return running + tile_image(
            stacked, inverse_rows, spectra_here, inverse_power(spectra_here), subspace_here
        )

    return lax.fori_loop(0, turns, add_block, accumulated)


def local(counts, subspace):
    spectra = make_spectra(counts)
    own_inverse = inverse_power(spectra)
    spectra_group, krylov_cluster = (
        lax.all_gather(spectra, "row", axis=0, tiled=True),
        lax.all_gather(subspace, "row", axis=0, tiled=True),
    )
    stacked = jnp.concatenate([spectra, twist(spectra)], axis=0)
    starting = jnp.zeros((spectra.shape[0], MODES), jnp.float32)
    projected = fold_pieces(
        starting,
        stacked,
        own_inverse,
        (
            lax.all_gather(spectra_group, "blk", axis=0, tiled=True),
            lax.all_gather(krylov_cluster, "blk", axis=0, tiled=True),
        ),
    )
    local_gram = jnp.dot(
        projected.T, projected, precision=lax.Precision.HIGHEST, preferred_element_type=jnp.float32
    )
    gram = lax.psum(local_gram, ("row", "blk"))
    factor = jnp.linalg.cholesky(gram)
    solved = jax.scipy.linalg.solve_triangular(factor, projected.T, lower=True)
    neuron_total = counts.shape[0] * lax.axis_size("row") * lax.axis_size("blk")
    return solved.T * jnp.sqrt(jnp.float32(neuron_total))


def solution(mesh):
    return jax.shard_map(
        local,
        mesh=mesh,
        in_specs=(P(("freq", "row", "blk"), None, None), P(("freq", "row", "blk"), None)),
        out_specs=P(("freq", "row", "blk"), None),
        check_vma=False,
    )
```

profile of v0, /device:TPU:16, one launch (start us, length us, event | category | flops | bytes accessed | tf_op | source)
XLA Modules:
  0.0 858.9 jit_solution(9733286293312651842)
XLA Ops:
  6.5 0.9 copy.24
  7.5 6.2 all_gather.14
  13.8 1.6 convert_reduce_fusion
  15.6 1.2 multiply_reduce_fusion.1
  17.0 0.3 convert_element_type.40
  17.4 6.3 all_gather.12
  23.7 1.2 convert_element_type.41
  25.8 88.7 %all-gather.5.cloned.1.call-done = bf16[32768,32]{1,0:T(8,128)(2,1)} async-done(((bf16[1024,32]{1,0:T(8,128)(2,1)}), bf16[32768,32]{1,0:T(8,128)(2,1)}) %all-gather.5.cloned.1.call-update) | async-done | bytes 2097168 | tf_op jit(solution)/shard_map/all_gather | solution.py:106
  114.5 97.5 %all-gather.3.cloned.1.call-done = bf16[32768,128]{1,0:T(8,128)(2,1)} async-done(((bf16[1024,128]{1,0:T(8,128)(2,1)}), bf16[32768,128]{1,0:T(8,128)(2,1)}) %all-gather.3.cloned.1.call-update) | async-done | bytes 8388624 | tf_op jit(solution)/shard_map/all_gather | solution.py:105
  212.0 82.8 %while.16 = (s32[]{:T(128)}, f32[256,32]{0,1:T(8,128)S(1)}, bf16[32768,128]{1,0:T(8,128)(2,1)}, bf16[512,128]{1,0:T(8,128)(2,1)S(1)}, f32[256]{0:T(256)S(1)}, /*...) while((s32[]{:T(128)}, f32[256,32]{0,1:T(8,128)S(1)}, ...), condition=%wide.region_5.0_spmd.clone, body=%wide.region_3.5_spmd.clone.sunk | while | flops 308037632 | bytes 10192049 | solution.py:88
  212.0 1.4 multiply_reduce_fusion.3
  213.4 1.7 convolution_bitcast_fusion.2
  215.1 2.0 convolution_add_fusion.2
  217.1 1.4 multiply_reduce_fusion.3
  218.6 1.8 convolution_bitcast_fusion.2
  220.3 2.0 convolution_add_fusion.2
  222.3 1.4 multiply_reduce_fusion.3
  223.7 1.8 convolution_bitcast_fusion.2
  225.5 2.0 convolution_add_fusion.2
  227.5 1.4 multiply_reduce_fusion.3
  228.9 1.7 convolution_bitcast_fusion.2
  230.7 2.0 convolution_add_fusion.2
  232.7 1.4 multiply_reduce_fusion.3
  234.1 1.8 convolution_bitcast_fusion.2
  235.8 2.0 convolution_add_fusion.2
  237.9 1.4 multiply_reduce_fusion.3
  239.3 1.8 convolution_bitcast_fusion.2
  241.0 2.0 convolution_add_fusion.2
  243.0 1.4 multiply_reduce_fusion.3
  244.4 1.7 convolution_bitcast_fusion.2
  246.2 2.0 convolution_add_fusion.2
  248.2 1.4 multiply_reduce_fusion.3
  249.6 1.8 convolution_bitcast_fusion.2
  251.4 2.0 convolution_add_fusion.2
  253.4 1.4 multiply_reduce_fusion.3
  254.8 1.8 convolution_bitcast_fusion.2
  256.6 2.0 convolution_add_fusion.2
  258.6 1.4 multiply_reduce_fusion.3
  260.0 1.7 convolution_bitcast_fusion.2
  261.7 2.0 convolution_add_fusion.2
  263.8 1.4 multiply_reduce_fusion.3
  265.2 1.8 convolution_bitcast_fusion.2
  266.9 2.0 convolution_add_fusion.2
  268.9 1.4 multiply_reduce_fusion.3
  270.3 1.8 convolution_bitcast_fusion.2
  272.1 2.0 convolution_add_fusion.2
  274.1 1.4 multiply_reduce_fusion.3
  275.5 1.7 convolution_bitcast_fusion.2
  277.3 2.0 convolution_add_fusion.2
  279.3 1.4 multiply_reduce_fusion.3
  280.7 1.8 convolution_bitcast_fusion.2
  282.5 2.0 convolution_add_fusion.2
  284.5 1.4 multiply_reduce_fusion.3
  285.9 1.8 convolution_bitcast_fusion.2
  287.6 2.0 convolution_add_fusion.2
  289.7 1.4 multiply_reduce_fusion.3
  291.1 1.7 convolution_bitcast_fusion.2
  292.8 2.0 convolution_add_fusion.2
  295.0 549.4 %psum.7 = f32[32,32]{0,1:T(8,128)S(1)} all-reduce(f32[32,32]{0,1:T(8,128)S(1)} %fusion.31), channel_id=1, replica_groups=mesh['freq'=2,'row'=4,'blk'=32] {'row','blk'}, use_global_device_ids=true, to_apply=%region_6.7 | all-reduce | flops 1024 | bytes 8192 | tf_op jit(solution)/shard_map/psum | solution.py:112
  844.5 2.9 cholesky.16
  847.4 0.6 compare_reduce_fusion
  848.1 0.7 fusion.21
  848.7 2.4 custom-call.7
  851.1 0.9 convolution_multiply_fusion
  (43 shorter events, 1.7 us)
Async XLA Ops:
  6.5 9.0 %copy-start = (s32[256,8,128]{2,1,0:T(8,128)S(1)}, s32[256,8,128]{2,1,0:T(8,128)}, u32[]{:S(2)}) copy-start(s32[256,8,128]{2,1,0:T(8,128)} %param.4) | copy-start | bytes 3145732
  6.5 107.9 %all-gather.5.cloned.1.call-start = ((), (), s32[]{:S(2)}) async-start(), calls=%async_computation.1 | async-start | bytes 8650752 | tf_op jit(solution)/shard_map/all_gather | solution.py:106
  13.7 198.3 %all-gather.3.cloned.1.call-start = ((), (), s32[]{:S(2)}) async-start(), calls=%async_computation | async-start | bytes 8650752 | tf_op jit(solution)/shard_map/all_gather | solution.py:105
Sparse Core Ops, SparseCore 0:
  13.8 100.5 all-gather.4
  117.0 94.8 all-gather.2
where the time goes:
time: 861 us; the launch traced here: 859 us
  blocking collectives  562 us (65%)
  waiting for transfers between devices  186 us (22%)
  matrix products  62 us (7%)
  other arithmetic  30.9 us (4%)
  between operations  13.6 us (2%)
    psum x1, blocking collectives, local(): gram = lax.psum(local_gram, ('row', 'blk'))  549 us
    all_gather x1, waiting for transfers between devices, local(): lax.all_gather(spectra_group, 'blk', axis=0, tiled=True)  97.5 us
    all_gather x1, waiting for transfers between devices, local(): lax.all_gather(krylov_cluster, 'blk', axis=0, tiled=True)  88.7 us
    dot_general x16, matrix products, tile_image(): jnp.dot(coherence, column_subspace, preferred_element_type=jnp.float32)  31.8 us
    dot_general x16, matrix products, tile_image(): lax.dot_general(stacked, column_spectra, (((1,), (1,)), ((), ())), prefer...  28 us
    reduce_sum x17, other arithmetic, inverse_power(): return 1.0 / (jnp.sum(widened * widened, axis=1) + 1e-05)  22.3 us
  transfers between devices with their start and end apart: 2, of which 2 were waited for; matrix products, arithmetic and copies ran while one was open for 1% of the time, Pallas kernels for 0%

commit v1 on v0

--- a/solution.py
+++ b/solution.py
@@ -109,7 +109,7 @@
     local_gram = jnp.dot(
         projected.T, projected, precision=lax.Precision.HIGHEST, preferred_element_type=jnp.float32
     )
-    gram = lax.psum(local_gram, ("row", "blk"))
+    gram = lax.psum(lax.psum(local_gram, "row"), "blk")
     factor = jnp.linalg.cholesky(gram)
     solved = jax.scipy.linalg.solve_triangular(factor, projected.T, lower=True)
     neuron_total = counts.shape[0] * lax.axis_size("row") * lax.axis_size("blk")

time: 861 us -> 462 us (0.54)
  blocking collectives: 562 us -> 162 us
    psum x1 -> x2, blocking collectives: 549 us -> 149 us  [local(): gram = lax.psum(lax.psum(local_gram, 'row'), 'blk')]
where the time goes in v1:
time: 462 us; the launch traced here: 459 us
  waiting for transfers between devices  186 us (40%)
  blocking collectives  162 us (35%)
  matrix products  62 us (13%)
  other arithmetic  30.9 us (7%)
  between operations  13.6 us (3%)
    psum x2, blocking collectives, local(): gram = lax.psum(lax.psum(local_gram, 'row'), 'blk')  149 us
    all_gather x1, waiting for transfers between devices, local(): lax.all_gather(spectra_group, 'blk', axis=0, tiled=True)  97.5 us
    all_gather x1, waiting for transfers between devices, local(): lax.all_gather(krylov_cluster, 'blk', axis=0, tiled=True)  88.7 us
    dot_general x16, matrix products, tile_image(): jnp.dot(coherence, column_subspace, preferred_element_type=jnp.float32)  31.8 us
    dot_general x16, matrix products, tile_image(): lax.dot_general(stacked, column_spectra, (((1,), (1,)), ((), ())), prefer...  28 us
    reduce_sum x17, other arithmetic, inverse_power(): return 1.0 / (jnp.sum(widened * widened, axis=1) + 1e-05)  22.3 us
  transfers between devices with their start and end apart: 2, of which 2 were waited for; matrix products, arithmetic and copies ran while one was open for 1% of the time, Pallas kernels for 0%

profile of v1, /device:TPU:16, one launch (start us, length us, event | category | flops | bytes accessed | tf_op | source)
XLA Modules:
  0.0 458.9 jit_solution(12641999017938806427)
XLA Ops:
  6.5 0.9 copy.24
  7.5 6.2 %all_gather.14 = bf16[1024,32]{1,0:T(8,128)(2,1)} all-gather(bf16[256,32]{1,0:T(8,128)(2,1)S(1)} %copy.24), channel_id=1, replica_groups=mesh['freq'=2,'row'=4,'blk'=32] {'row'}, dimensions={0}, use_global_device_ids=true | all-gather | bytes 81920 | tf_op jit(solution)/shard_map/all_gather | solution.py:96
  13.8 1.6 convert_reduce_fusion
  15.6 1.2 multiply_reduce_fusion.1
  17.4 6.3 %all_gather.12 = bf16[1024,128]{1,0:T(8,128)(2,1)} all-gather(bf16[256,128]{1,0:T(8,128)(2,1)S(1)} %convert_element_type.40), channel_id=1, replica_groups=mesh['freq'=2,'row'=4,'blk'=32] {'row'}, dimensions={0}, use_global_device_ids=true | all-gather | bytes 327680 | tf_op jit(solution)/shard_map/all_gather | solution.py:95
  23.7 1.2 convert_element_type.41
  25.8 88.7 %all-gather.5.cloned.1.call-done = bf16[32768,32]{1,0:T(8,128)(2,1)} async-done(((bf16[1024,32]{1,0:T(8,128)(2,1)}), bf16[32768,32]{1,0:T(8,128)(2,1)}) %all-gather.5.cloned.1.call-update) | async-done | bytes 2097168 | tf_op jit(solution)/shard_map/all_gather | solution.py:106
  114.5 97.5 %all-gather.3.cloned.1.call-done = bf16[32768,128]{1,0:T(8,128)(2,1)} async-done(((bf16[1024,128]{1,0:T(8,128)(2,1)}), bf16[32768,128]{1,0:T(8,128)(2,1)}) %all-gather.3.cloned.1.call-update) | async-done | bytes 8388624 | tf_op jit(solution)/shard_map/all_gather | solution.py:105
  212.0 82.8 %while.16 = (s32[]{:T(128)}, f32[256,32]{0,1:T(8,128)S(1)}, bf16[32768,128]{1,0:T(8,128)(2,1)}, bf16[512,128]{1,0:T(8,128)(2,1)S(1)}, f32[256]{0:T(256)S(1)}, /*...) while((s32[]{:T(128)}, f32[256,32]{0,1:T(8,128)S(1)}, ...), condition=%wide.region_5.0_spmd.clone, body=%wide.region_3.5_spmd.clone.sunk | while | flops 308037632 | bytes 10192049 | solution.py:88
  212.0 1.4 multiply_reduce_fusion.3
  213.4 1.7 convolution_bitcast_fusion.2
  215.1 2.0 convolution_add_fusion.2
  217.1 1.4 multiply_reduce_fusion.3
  218.6 1.8 convolution_bitcast_fusion.2
  220.3 2.0 convolution_add_fusion.2
  222.3 1.4 multiply_reduce_fusion.3
  223.7 1.8 convolution_bitcast_fusion.2
  225.5 2.0 convolution_add_fusion.2
  227.5 1.4 multiply_reduce_fusion.3
  228.9 1.7 convolution_bitcast_fusion.2
  230.7 2.0 convolution_add_fusion.2
  232.7 1.4 multiply_reduce_fusion.3
  234.1 1.8 convolution_bitcast_fusion.2
  235.8 2.0 convolution_add_fusion.2
  237.9 1.4 multiply_reduce_fusion.3
  239.3 1.8 convolution_bitcast_fusion.2
  241.0 2.0 convolution_add_fusion.2
  243.0 1.4 multiply_reduce_fusion.3
  244.4 1.7 convolution_bitcast_fusion.2
  246.2 2.0 convolution_add_fusion.2
  248.2 1.4 multiply_reduce_fusion.3
  249.6 1.8 convolution_bitcast_fusion.2
  251.4 2.0 convolution_add_fusion.2
  253.4 1.4 multiply_reduce_fusion.3
  254.8 1.8 convolution_bitcast_fusion.2
  256.6 2.0 convolution_add_fusion.2
  258.6 1.4 multiply_reduce_fusion.3
  260.0 1.7 convolution_bitcast_fusion.2
  261.7 2.0 convolution_add_fusion.2
  263.8 1.4 multiply_reduce_fusion.3
  265.2 1.8 convolution_bitcast_fusion.2
  266.9 2.0 convolution_add_fusion.2
  268.9 1.4 multiply_reduce_fusion.3
  270.3 1.8 convolution_bitcast_fusion.2
  272.1 2.0 convolution_add_fusion.2
  274.1 1.4 multiply_reduce_fusion.3
  275.5 1.7 convolution_bitcast_fusion.2
  277.3 2.0 convolution_add_fusion.2
  279.3 1.4 multiply_reduce_fusion.3
  280.7 1.8 convolution_bitcast_fusion.2
  282.5 2.0 convolution_add_fusion.2
  284.5 1.4 multiply_reduce_fusion.3
  285.9 1.8 convolution_bitcast_fusion.2
  287.6 2.0 convolution_add_fusion.2
  289.7 1.4 multiply_reduce_fusion.3
  291.1 1.7 convolution_bitcast_fusion.2
  292.8 2.0 convolution_add_fusion.2
  295.0 10.1 %psum.14 = f32[32,32]{0,1:T(8,128)S(1)} all-reduce(f32[32,32]{0,1:T(8,128)S(1)} %fusion.31), channel_id=1, replica_groups=mesh['freq'=2,'row'=4,'blk'=32] {'row'}, use_global_device_ids=true, to_apply=%region_6.0 | all-reduce | flops 1024 | bytes 8192 | tf_op jit(solution)/shard_map/psum | solution.py:112
  305.1 139.3 %psum.15 = f32[32,32]{0,1:T(8,128)S(1)} all-reduce(f32[32,32]{0,1:T(8,128)S(1)} %psum.14), channel_id=1, replica_groups=mesh['freq'=2,'row'=4,'blk'=32] {'blk'}, use_global_device_ids=true, to_apply=%region_7.8 | all-reduce | flops 1024 | bytes 8192 | tf_op jit(solution)/shard_map/psum | solution.py:112
  444.5 2.9 cholesky.16
  447.4 0.6 compare_reduce_fusion
  448.1 0.7 fusion.21
  448.7 2.4 custom-call.7
  451.2 0.9 convolution_multiply_fusion
  (44 shorter events, 2.1 us)
Async XLA Ops:
  6.5 9.0 %copy-start = (s32[256,8,128]{2,1,0:T(8,128)S(1)}, s32[256,8,128]{2,1,0:T(8,128)}, u32[]{:S(2)}) copy-start(s32[256,8,128]{2,1,0:T(8,128)} %param.4) | copy-start | bytes 3145732
  6.5 107.9 %all-gather.5.cloned.1.call-start = ((), (), s32[]{:S(2)}) async-start(), calls=%async_computation.1 | async-start | bytes 8650752 | tf_op jit(solution)/shard_map/all_gather | solution.py:106
  13.7 198.3 %all-gather.3.cloned.1.call-start = ((), (), s32[]{:S(2)}) async-start(), calls=%async_computation | async-start | bytes 8650752 | tf_op jit(solution)/shard_map/all_gather | solution.py:105
Sparse Core Ops, SparseCore 0:
  13.8 100.5 all-gather.4
  117.0 94.8 all-gather.2
